TPU v7x, 512 devices: a whole 4x8x8 slice. The times are simulated.
512 devices in a mesh: blk: 64 (over y, x, z_lo), rep: 8 (over z_hi, core).
Axes of the slice: x: 4, y: 8, z: 8 (z_hi: 4, z_lo: 2; z = z_hi * 2 + z_lo), core: 2. Of those that a mesh axis runs over, the one named last changes fastest.
Arguments:
- features: bfloat16 [65536, 256], P(('blk', 'rep')), may hold values from -6 to 6
- degrees: int32 [65536], P(('blk', 'rep')), may hold values from 4 to 64
- tile_values: bfloat16 [512, 16, 8, 128, 128], P(('blk', 'rep')), may hold values from 0 to 1
- tile_rows: int32 [512, 16, 8], P(('blk', 'rep')), may hold values from 0 to 7, as said below
- tile_counts: int32 [512, 16], P(('blk', 'rep')), may hold values from 1 to 8, as said below
- weight: bfloat16 [256, 256], replicated, may hold values from -0.375 to 0.375
- cotangent: bfloat16 [65536, 256], P(('blk', 'rep')), may hold values from -6 to 6
Outputs:
- activations: bfloat16 [65536, 256], P(('blk', 'rep'))
- grad_weight: float32 [256, 256], replicated
- grad_features: bfloat16 [65536, 256], P(('blk', 'rep'))
Inputs may be any that keep to these rules, and one draw needn't show every extreme that they name: `tile_rows`: the 8 slots of one owner and distance name the 8 row blocks of its slab, each once. Only the first tile_counts[o, s] slots of owner o and distance s are live. In every draw some slab has all 8 slots live at every distance for every owner in it.
All inputs are finite; a program needn't handle non-finite values.
Results may differ from a plain program's by a relative error of at most 0.0077.
Values may be sent and summed in bfloat16 or wider, within the bound.
No kernel may reach another device: no remote copies, remote signals or barrier semaphores. Data moves between devices by JAX's collectives and lax.ppermute only.
A program may use at most 64 MiB of HBM per device.

v0:
```python
import math
import jax
import jax.numpy as jnp
from jax import lax
from jax.sharding import PartitionSpec as P


def passed_along(block, axis, distance):
    devices = range(lax.axis_size(axis))
    route = [((i - distance) % len(devices), i) for i in devices]
    return lax.ppermute(block, axis, route)


def per_device(features, degrees, tile_values, tile_rows, tile_counts, weight, cotangent):
    own_rows = features.shape[0]
    feature_width = features.shape[1]
    span_count = tile_values.shape[1]
    slot_count = tile_values.shape[2]
    block_size = tile_values.shape[3]
    inv_root = lax.rsqrt(degrees.astype(jnp.float32))[:, None]
    scaled = (features.astype(jnp.float32) * inv_root).astype(jnp.bfloat16)
    tile_stack = tile_values[0]
    row_stack = tile_rows[0]
    count_stack = tile_counts[0]
    slot_ids = jnp.arange(slot_count, dtype=jnp.int32)

    def load_distance(distance):
        tile_block = lax.dynamic_index_in_dim(tile_stack, distance, 0, keepdims=False)
        row_ids = lax.dynamic_index_in_dim(row_stack, distance, 0, keepdims=False)
        live_count = lax.dynamic_index_in_dim(count_stack, distance, 0, keepdims=False)
        return (tile_block, row_ids, live_count)

    def gather_rows(partial_sum, distance, source_rows):
        tile_block, row_ids, live_count = load_distance(distance)
        match_table = row_ids[None, :] == slot_ids[:, None]
        slot_of_row = jnp.sum(jnp.where(match_table, slot_ids[None, :], 0), axis=1)
        arranged = jnp.take(tile_block, slot_of_row, axis=0)
        row_live = slot_of_row < live_count
        product = jnp.einsum(
            "mij,jf->mif", arranged, source_rows, preferred_element_type=jnp.float32
        )
        return partial_sum + jnp.where(row_live[:, None, None], product, 0.0)

    def forward_turn(distance, carry):
        partial_sum, source_rows = carry
        partial_sum = gather_rows(partial_sum, distance, source_rows)
        source_rows = passed_along(source_rows, "blk", 1)
        return (partial_sum, source_rows)

    start_total = jnp.zeros((slot_count, block_size, feature_width), jnp.float32)
    partial_sum, source_rows = lax.fori_loop(0, span_count - 1, forward_turn, (start_total, scaled))
    partial_sum = gather_rows(partial_sum, span_count - 1, source_rows)
    slab_partial = partial_sum.reshape(slot_count * block_size, feature_width)
    own_sum = lax.psum_scatter(slab_partial, "rep", scatter_dimension=0, tiled=True)
    aggregated = (own_sum * inv_root).astype(jnp.bfloat16)
    pre_act = jnp.dot(aggregated, weight, preferred_element_type=jnp.float32)
    sigma = jax.nn.sigmoid(pre_act)
    activations = (pre_act * sigma).astype(jnp.bfloat16)
    act_grad = (cotangent.astype(jnp.float32) * sigma * (1.0 + pre_act * (1.0 - sigma))).astype(
        jnp.bfloat16
    )
    local_weight = lax.dot_general(
        aggregated, act_grad, (((0,), (0,)), ((), ())), preferred_element_type=jnp.float32
    )
    node_total = own_rows * lax.axis_size("blk") * lax.axis_size("rep")
    grad_weight = lax.psum(local_weight, ("blk", "rep")) / math.sqrt(node_total)
    back_grad = lax.dot_general(
        act_grad, weight, (((1,), (1,)), ((), ())), preferred_element_type=jnp.float32
    )
    back_scaled = (back_grad * inv_root).astype(jnp.bfloat16)
    slab_grads = lax.all_gather(back_scaled, "rep", axis=0, tiled=True).reshape(
        slot_count, block_size, feature_width
    )

    def scatter_rows(back_sum, distance):
        tile_block, row_ids, live_count = load_distance(distance)
        picked = jnp.take(slab_grads, row_ids, axis=0)
        picked = jnp.where((slot_ids < live_count)[:, None, None], picked, jnp.zeros_like(picked))
        return back_sum + jnp.einsum(
            "kij,kif->jf", tile_block, picked, preferred_element_type=jnp.float32
        )

    def backward_turn(turn_index, back_sum):
        back_sum = scatter_rows(back_sum, span_count - 1 - turn_index)
        return passed_along(back_sum, "blk", -1)

    zero_back = jnp.zeros((own_rows, feature_width), jnp.float32)
    back_total = lax.fori_loop(0, span_count - 1, backward_turn, zero_back)
    back_total = scatter_rows(back_total, 0)
    grad_features = (back_total * inv_root).astype(jnp.bfloat16)
    return (activations, grad_weight, grad_features)


def solution(mesh):
    placed = (
        P(("blk", "rep"), None),
        P(("blk", "rep")),
        P(("blk", "rep"), None, None, None, None),
        P(("blk", "rep"), None, None),
        P(("blk", "rep"), None),
        P(),
        P(("blk", "rep"), None),
    )
    return jax.shard_map(
        per_device,
        mesh=mesh,
        in_specs=placed,
        out_specs=(P(("blk", "rep"), None), P(), P(("blk", "rep"), None)),
        check_vma=False,
    )
```

profile of v0, /device:TPU:23, one launch (start us, length us, event | category | flops | bytes accessed | tf_op | source)
XLA Modules:
  0.0 516.1 jit_solution(8821793906793815661)
XLA Ops:
  9.8 1.3 fusion.41
  14.3 121.5 %while.34 = (s32[]{:T(128)}, f32[8,128,256]{2,1,0:T(8,128)S(1)}, bf16[128,256]{1,0:T(8,128)(2,1)S(1)}, s32[16,8]{1,0:T(8,128)S(1)}, s32[16]{0:T(128)}, /*index=5...) while((s32[]{:T(128)}, f32[8,128,256]{2,1,0:T(8,128)S(1)}, ...), condition=%wide.region_2.4_spmd.clone.clone, body=%wide.region_0.3_spmd.clone.clone.sunk | while | flops 68027656 | bytes 3871199 | solution.py:51
  14.3 4.0 collective-permute-start.1
  22.6 2.2 collective-permute-start.1
  29.2 4.0 collective-permute-start.1
  37.5 3.7 collective-permute-start.1
  45.6 3.7 collective-permute-start.1
  53.6 3.7 collective-permute-start.1
  61.6 3.7 collective-permute-start.1
  69.6 3.7 collective-permute-start.1
  77.6 3.7 collective-permute-start.1
  85.6 4.1 collective-permute-start.1
  94.0 3.7 collective-permute-start.1
  102.0 3.7 collective-permute-start.1
  110.0 3.7 collective-permute-start.1
  118.1 4.2 collective-permute-start.1
  126.6 4.9 collective-permute-start.1
  135.8 1.3 fusion.21
  137.9 77.7 %reduce-scatter.2.cloned.1.call-done = f32[128,256]{1,0:T(8,128)} async-done(((f32[1024,256]{1,0:T(8,128)}), f32[128,256]{1,0:T(8,128)}) %reduce-scatter.2.cloned.1.call-update) | async-done | bytes 131088 | tf_op jit(solution)/shard_map/reduce_scatter | solution.py:54
  215.6 1.8 multiply_convert_fusion
  217.6 17.1 %all_gather.3 = bf16[1024,256]{1,0:T(8,128)(2,1)S(1)} all-gather(bf16[128,256]{1,0:T(8,128)(2,1)S(1)} %fusion.25), channel_id=1, replica_groups=mesh['blk'=64,'rep'=8] {'rep'}, dimensions={0}, use_global_device_ids=true | all-gather | bytes 589824 | tf_op jit(solution)/shard_map/all_gather | solution.py:71
  234.7 1.9 fusion.39
  237.3 179.3 %while.33 = (s32[]{:T(128)}, f32[128,256]{1,0:T(8,128)S(1)}, bf16[16,8,128,128]{3,2,1,0:T(8,128)(2,1)}, s32[16]{0:T(128)S(1)}, s32[16,8]{1,0:T(8,128)S(1)}, /*in...) while((s32[]{:T(128)}, f32[128,256]{1,0:T(8,128)S(1)}, ...), condition=%wide.region_7.10_spmd.clone, body=%wide.region_6.9_spmd.clone.sunk | while | flops 67667008 | bytes 2625907 | solution.py:88
  240.6 2.1 collective-permute-start
  242.7 4.7 collective-permute-done
  249.3 1.3 fusion.53
  250.6 3.0 collective-permute-start
  253.6 4.8 collective-permute-done
  260.4 1.3 fusion.53
  261.6 1.9 collective-permute-start
  263.6 6.5 %collective-permute-done = f32[128,256]{1,0:T(8,128)S(1)} collective-permute-done((f32[128,256]{1,0:T(8,128)S(1)}, f32[128,256]{1,0:T(8,128)S(1)}, u32[]{:S(2)}, u32[]{:S(2)}) %collective-permute-start) | collective-permute-done | bytes 131104 | tf_op jit(solution)/shard_map/while/body/eval_jaxpr/ppermute | solution.py:11
  273.3 1.9 collective-permute-start
  275.3 6.8 %collective-permute-done = f32[128,256]{1,0:T(8,128)S(1)} collective-permute-done((f32[128,256]{1,0:T(8,128)S(1)}, f32[128,256]{1,0:T(8,128)S(1)}, u32[]{:S(2)}, u32[]{:S(2)}) %collective-permute-start) | collective-permute-done | bytes 131104 | tf_op jit(solution)/shard_map/while/body/eval_jaxpr/ppermute | solution.py:11
  285.3 1.9 collective-permute-start
  287.2 6.7 %collective-permute-done = f32[128,256]{1,0:T(8,128)S(1)} collective-permute-done((f32[128,256]{1,0:T(8,128)S(1)}, f32[128,256]{1,0:T(8,128)S(1)}, u32[]{:S(2)}, u32[]{:S(2)}) %collective-permute-start) | collective-permute-done | bytes 131104 | tf_op jit(solution)/shard_map/while/body/eval_jaxpr/ppermute | solution.py:11
  295.9 1.3 fusion.53
  297.2 1.9 collective-permute-start
  299.1 6.7 %collective-permute-done = f32[128,256]{1,0:T(8,128)S(1)} collective-permute-done((f32[128,256]{1,0:T(8,128)S(1)}, f32[128,256]{1,0:T(8,128)S(1)}, u32[]{:S(2)}, u32[]{:S(2)}) %collective-permute-start) | collective-permute-done | bytes 131104 | tf_op jit(solution)/shard_map/while/body/eval_jaxpr/ppermute | solution.py:11
  309.1 1.9 collective-permute-start
  311.0 7.2 %collective-permute-done = f32[128,256]{1,0:T(8,128)S(1)} collective-permute-done((f32[128,256]{1,0:T(8,128)S(1)}, f32[128,256]{1,0:T(8,128)S(1)}, u32[]{:S(2)}, u32[]{:S(2)}) %collective-permute-start) | collective-permute-done | bytes 131104 | tf_op jit(solution)/shard_map/while/body/eval_jaxpr/ppermute | solution.py:11
  320.2 1.3 fusion.53
  321.5 1.9 collective-permute-start
  323.4 6.9 %collective-permute-done = f32[128,256]{1,0:T(8,128)S(1)} collective-permute-done((f32[128,256]{1,0:T(8,128)S(1)}, f32[128,256]{1,0:T(8,128)S(1)}, u32[]{:S(2)}, u32[]{:S(2)}) %collective-permute-start) | collective-permute-done | bytes 131104 | tf_op jit(solution)/shard_map/while/body/eval_jaxpr/ppermute | solution.py:11
  333.6 1.9 collective-permute-start
  335.5 6.3 %collective-permute-done = f32[128,256]{1,0:T(8,128)S(1)} collective-permute-done((f32[128,256]{1,0:T(8,128)S(1)}, f32[128,256]{1,0:T(8,128)S(1)}, u32[]{:S(2)}, u32[]{:S(2)}) %collective-permute-start) | collective-permute-done | bytes 131104 | tf_op jit(solution)/shard_map/while/body/eval_jaxpr/ppermute | solution.py:11
  343.8 1.3 fusion.53
  345.1 1.9 collective-permute-start
  347.1 7.2 %collective-permute-done = f32[128,256]{1,0:T(8,128)S(1)} collective-permute-done((f32[128,256]{1,0:T(8,128)S(1)}, f32[128,256]{1,0:T(8,128)S(1)}, u32[]{:S(2)}, u32[]{:S(2)}) %collective-permute-start) | collective-permute-done | bytes 131104 | tf_op jit(solution)/shard_map/while/body/eval_jaxpr/ppermute | solution.py:11
  356.2 1.3 fusion.53
  357.5 1.9 collective-permute-start
  359.5 6.6 %collective-permute-done = f32[128,256]{1,0:T(8,128)S(1)} collective-permute-done((f32[128,256]{1,0:T(8,128)S(1)}, f32[128,256]{1,0:T(8,128)S(1)}, u32[]{:S(2)}, u32[]{:S(2)}) %collective-permute-start) | collective-permute-done | bytes 131104 | tf_op jit(solution)/shard_map/while/body/eval_jaxpr/ppermute | solution.py:11
  368.1 1.3 fusion.53
  369.3 1.9 collective-permute-start
  371.3 8.0 %collective-permute-done = f32[128,256]{1,0:T(8,128)S(1)} collective-permute-done((f32[128,256]{1,0:T(8,128)S(1)}, f32[128,256]{1,0:T(8,128)S(1)}, u32[]{:S(2)}, u32[]{:S(2)}) %collective-permute-start) | collective-permute-done | bytes 131104 | tf_op jit(solution)/shard_map/while/body/eval_jaxpr/ppermute | solution.py:11
  381.2 1.3 fusion.53
  382.5 1.9 collective-permute-start
  384.4 8.5 %collective-permute-done = f32[128,256]{1,0:T(8,128)S(1)} collective-permute-done((f32[128,256]{1,0:T(8,128)S(1)}, f32[128,256]{1,0:T(8,128)S(1)}, u32[]{:S(2)}, u32[]{:S(2)}) %collective-permute-start) | collective-permute-done | bytes 131104 | tf_op jit(solution)/shard_map/while/body/eval_jaxpr/ppermute | solution.py:11
  396.2 1.9 collective-permute-start
  398.2 6.4 %collective-permute-done = f32[128,256]{1,0:T(8,128)S(1)} collective-permute-done((f32[128,256]{1,0:T(8,128)S(1)}, f32[128,256]{1,0:T(8,128)S(1)}, u32[]{:S(2)}, u32[]{:S(2)}) %collective-permute-start) | collective-permute-done | bytes 131104 | tf_op jit(solution)/shard_map/while/body/eval_jaxpr/ppermute | solution.py:11
  407.8 1.9 collective-permute-start
  409.8 6.8 %collective-permute-done = f32[128,256]{1,0:T(8,128)S(1)} collective-permute-done((f32[128,256]{1,0:T(8,128)S(1)}, f32[128,256]{1,0:T(8,128)S(1)}, u32[]{:S(2)}, u32[]{:S(2)}) %collective-permute-start) | collective-permute-done | bytes 131104 | tf_op jit(solution)/shard_map/while/body/eval_jaxpr/ppermute | solution.py:11
  416.6 1.9 fusion.24
  418.5 89.1 %all-reduce.2.cloned.1.call-done = f32[256,256]{1,0:T(8,128)} async-done(((f32[256,256]{1,0:T(8,128)}), f32[256,256]{1,0:T(8,128)}) %all-reduce.2.cloned.1.call-update) | async-done | bytes 262160 | tf_op jit(solution)/shard_map/psum | solution.py:66
  507.6 1.7 broadcast_multiply_fusion
  (259 shorter events, 109.3 us)
Async XLA Ops:
  7.2 208.5 %copy-start = (bf16[256,256]{1,0:T(8,128)(2,1)S(1)}, bf16[256,256]{1,0:T(8,128)(2,1)}, u32[]{:S(2)}) copy-start(bf16[256,256]{1,0:T(8,128)(2,1)} %param.20) | copy-start | bytes 393220
  7.2 208.4 %reduce-scatter.2.cloned.1.call-start = ((), (), s32[]{:S(2)}) async-start(), calls=%async_computation.1 | async-start | bytes 1179648 | tf_op jit(solution)/shard_map/reduce_scatter | solution.py:54
  14.3 201.4 %copy-start.2 = (bf16[128,256]{1,0:T(8,128)(2,1)S(1)}, bf16[128,256]{1,0:T(8,128)(2,1)}, u32[]{:S(2)}) copy-start(bf16[128,256]{1,0:T(8,128)(2,1)} %param.21) | copy-start | bytes 196612
  14.3 8.3 %collective-permute-start.1 = (bf16[128,256]{1,0:T(8,128)(2,1)S(1)}, bf16[128,256]{1,0:T(8,128)(2,1)S(1)}, u32[]{:S(2)}, u32[]{:S(2)}) collective-permute-start(bf16[128,256]{1,0:T(8,128)(2,1)S(1)} %copy.29), channel_id=1, source_target_pairs={{504,0},{0,8},{8,16},{16,24},{24,32},{32,40},{40,48},{48,56},{56,6... | collective-permute-start | bytes 196616 | tf_op jit(solution)/shard_map/while/body/eval_jaxpr/ppermute | solution.py:11
  22.6 6.5 %collective-permute-start.1 = (bf16[128,256]{1,0:T(8,128)(2,1)S(1)}, bf16[128,256]{1,0:T(8,128)(2,1)S(1)}, u32[]{:S(2)}, u32[]{:S(2)}) collective-permute-start(bf16[128,256]{1,0:T(8,128)(2,1)S(1)} %copy.29), channel_id=1, source_target_pairs={{504,0},{0,8},{8,16},{16,24},{24,32},{32,40},{40,48},{48,56},{56,6... | collective-permute-start | bytes 196616 | tf_op jit(solution)/shard_map/while/body/eval_jaxpr/ppermute | solution.py:11
  29.2 8.3 %collective-permute-start.1 = (bf16[128,256]{1,0:T(8,128)(2,1)S(1)}, bf16[128,256]{1,0:T(8,128)(2,1)S(1)}, u32[]{:S(2)}, u32[]{:S(2)}) collective-permute-start(bf16[128,256]{1,0:T(8,128)(2,1)S(1)} %copy.29), channel_id=1, source_target_pairs={{504,0},{0,8},{8,16},{16,24},{24,32},{32,40},{40,48},{48,56},{56,6... | collective-permute-start | bytes 196616 | tf_op jit(solution)/shard_map/while/body/eval_jaxpr/ppermute | solution.py:11
  37.5 8.0 %collective-permute-start.1 = (bf16[128,256]{1,0:T(8,128)(2,1)S(1)}, bf16[128,256]{1,0:T(8,128)(2,1)S(1)}, u32[]{:S(2)}, u32[]{:S(2)}) collective-permute-start(bf16[128,256]{1,0:T(8,128)(2,1)S(1)} %copy.29), channel_id=1, source_target_pairs={{504,0},{0,8},{8,16},{16,24},{24,32},{32,40},{40,48},{48,56},{56,6... | collective-permute-start | bytes 196616 | tf_op jit(solution)/shard_map/while/body/eval_jaxpr/ppermute | solution.py:11
  45.6 8.0 %collective-permute-start.1 = (bf16[128,256]{1,0:T(8,128)(2,1)S(1)}, bf16[128,256]{1,0:T(8,128)(2,1)S(1)}, u32[]{:S(2)}, u32[]{:S(2)}) collective-permute-start(bf16[128,256]{1,0:T(8,128)(2,1)S(1)} %copy.29), channel_id=1, source_target_pairs={{504,0},{0,8},{8,16},{16,24},{24,32},{32,40},{40,48},{48,56},{56,6... | collective-permute-start | bytes 196616 | tf_op jit(solution)/shard_map/while/body/eval_jaxpr/ppermute | solution.py:11
  53.6 8.0 %collective-permute-start.1 = (bf16[128,256]{1,0:T(8,128)(2,1)S(1)}, bf16[128,256]{1,0:T(8,128)(2,1)S(1)}, u32[]{:S(2)}, u32[]{:S(2)}) collective-permute-start(bf16[128,256]{1,0:T(8,128)(2,1)S(1)} %copy.29), channel_id=1, source_target_pairs={{504,0},{0,8},{8,16},{16,24},{24,32},{32,40},{40,48},{48,56},{56,6... | collective-permute-start | bytes 196616 | tf_op jit(solution)/shard_map/while/body/eval_jaxpr/ppermute | solution.py:11
  61.6 8.0 %collective-permute-start.1 = (bf16[128,256]{1,0:T(8,128)(2,1)S(1)}, bf16[128,256]{1,0:T(8,128)(2,1)S(1)}, u32[]{:S(2)}, u32[]{:S(2)}) collective-permute-start(bf16[128,256]{1,0:T(8,128)(2,1)S(1)} %copy.29), channel_id=1, source_target_pairs={{504,0},{0,8},{8,16},{16,24},{24,32},{32,40},{40,48},{48,56},{56,6... | collective-permute-start | bytes 196616 | tf_op jit(solution)/shard_map/while/body/eval_jaxpr/ppermute | solution.py:11
  69.6 8.0 %collective-permute-start.1 = (bf16[128,256]{1,0:T(8,128)(2,1)S(1)}, bf16[128,256]{1,0:T(8,128)(2,1)S(1)}, u32[]{:S(2)}, u32[]{:S(2)}) collective-permute-start(bf16[128,256]{1,0:T(8,128)(2,1)S(1)} %copy.29), channel_id=1, source_target_pairs={{504,0},{0,8},{8,16},{16,24},{24,32},{32,40},{40,48},{48,56},{56,6... | collective-permute-start | bytes 196616 | tf_op jit(solution)/shard_map/while/body/eval_jaxpr/ppermute | solution.py:11
  77.6 8.0 %collective-permute-start.1 = (bf16[128,256]{1,0:T(8,128)(2,1)S(1)}, bf16[128,256]{1,0:T(8,128)(2,1)S(1)}, u32[]{:S(2)}, u32[]{:S(2)}) collective-permute-start(bf16[128,256]{1,0:T(8,128)(2,1)S(1)} %copy.29), channel_id=1, source_target_pairs={{504,0},{0,8},{8,16},{16,24},{24,32},{32,40},{40,48},{48,56},{56,6... | collective-permute-start | bytes 196616 | tf_op jit(solution)/shard_map/while/body/eval_jaxpr/ppermute | solution.py:11
  85.6 8.4 %collective-permute-start.1 = (bf16[128,256]{1,0:T(8,128)(2,1)S(1)}, bf16[128,256]{1,0:T(8,128)(2,1)S(1)}, u32[]{:S(2)}, u32[]{:S(2)}) collective-permute-start(bf16[128,256]{1,0:T(8,128)(2,1)S(1)} %copy.29), channel_id=1, source_target_pairs={{504,0},{0,8},{8,16},{16,24},{24,32},{32,40},{40,48},{48,56},{56,6... | collective-permute-start | bytes 196616 | tf_op jit(solution)/shard_map/while/body/eval_jaxpr/ppermute | solution.py:11
  94.0 8.0 %collective-permute-start.1 = (bf16[128,256]{1,0:T(8,128)(2,1)S(1)}, bf16[128,256]{1,0:T(8,128)(2,1)S(1)}, u32[]{:S(2)}, u32[]{:S(2)}) collective-permute-start(bf16[128,256]{1,0:T(8,128)(2,1)S(1)} %copy.29), channel_id=1, source_target_pairs={{504,0},{0,8},{8,16},{16,24},{24,32},{32,40},{40,48},{48,56},{56,6... | collective-permute-start | bytes 196616 | tf_op jit(solution)/shard_map/while/body/eval_jaxpr/ppermute | solution.py:11
  102.0 8.0 %collective-permute-start.1 = (bf16[128,256]{1,0:T(8,128)(2,1)S(1)}, bf16[128,256]{1,0:T(8,128)(2,1)S(1)}, u32[]{:S(2)}, u32[]{:S(2)}) collective-permute-start(bf16[128,256]{1,0:T(8,128)(2,1)S(1)} %copy.29), channel_id=1, source_target_pairs={{504,0},{0,8},{8,16},{16,24},{24,32},{32,40},{40,48},{48,56},{56,6... | collective-permute-start | bytes 196616 | tf_op jit(solution)/shard_map/while/body/eval_jaxpr/ppermute | solution.py:11
  110.0 8.0 %collective-permute-start.1 = (bf16[128,256]{1,0:T(8,128)(2,1)S(1)}, bf16[128,256]{1,0:T(8,128)(2,1)S(1)}, u32[]{:S(2)}, u32[]{:S(2)}) collective-permute-start(bf16[128,256]{1,0:T(8,128)(2,1)S(1)} %copy.29), channel_id=1, source_target_pairs={{504,0},{0,8},{8,16},{16,24},{24,32},{32,40},{40,48},{48,56},{56,6... | collective-permute-start | bytes 196616 | tf_op jit(solution)/shard_map/while/body/eval_jaxpr/ppermute | solution.py:11
  118.1 8.5 %collective-permute-start.1 = (bf16[128,256]{1,0:T(8,128)(2,1)S(1)}, bf16[128,256]{1,0:T(8,128)(2,1)S(1)}, u32[]{:S(2)}, u32[]{:S(2)}) collective-permute-start(bf16[128,256]{1,0:T(8,128)(2,1)S(1)} %copy.29), channel_id=1, source_target_pairs={{504,0},{0,8},{8,16},{16,24},{24,32},{32,40},{40,48},{48,56},{56,6... | collective-permute-start | bytes 196616 | tf_op jit(solution)/shard_map/while/body/eval_jaxpr/ppermute | solution.py:11
  126.6 9.2 %collective-permute-start.1 = (bf16[128,256]{1,0:T(8,128)(2,1)S(1)}, bf16[128,256]{1,0:T(8,128)(2,1)S(1)}, u32[]{:S(2)}, u32[]{:S(2)}) collective-permute-start(bf16[128,256]{1,0:T(8,128)(2,1)S(1)} %copy.29), channel_id=1, source_target_pairs={{504,0},{0,8},{8,16},{16,24},{24,32},{32,40},{40,48},{48,56},{56,6... | collective-permute-start | bytes 196616 | tf_op jit(solution)/shard_map/while/body/eval_jaxpr/ppermute | solution.py:11
  135.8 101.5 %copy-start.1 = (s32[16]{0:T(128)S(1)}, s32[16]{0:T(128)}, u32[]{:S(2)}) copy-start(s32[16]{0:T(128)} %get-tuple-element.582) | copy-start | bytes 196
  137.2 370.4 %all-reduce.2.cloned.1.call-start = ((), (), s32[]{:S(2)}) async-start(), calls=%async_computation.2 | async-start | bytes 524288 | tf_op jit(solution)/shard_map/psum | solution.py:66
  240.6 6.8 %collective-permute-start = (f32[128,256]{1,0:T(8,128)S(1)}, f32[128,256]{1,0:T(8,128)S(1)}, u32[]{:S(2)}, u32[]{:S(2)}) collective-permute-start(f32[128,256]{1,0:T(8,128)S(1)} %fusion.53), channel_id=1, source_target_pairs={{8,0},{16,8},{24,16},{32,24},{40,32},{48,40},{56,48},{64,56},{72,6... | collective-permute-start | bytes 393224 | tf_op jit(solution)/shard_map/while/body/eval_jaxpr/ppermute | solution.py:11
  250.6 7.8 %collective-permute-start = (f32[128,256]{1,0:T(8,128)S(1)}, f32[128,256]{1,0:T(8,128)S(1)}, u32[]{:S(2)}, u32[]{:S(2)}) collective-permute-start(f32[128,256]{1,0:T(8,128)S(1)} %fusion.53), channel_id=1, source_target_pairs={{8,0},{16,8},{24,16},{32,24},{40,32},{48,40},{56,48},{64,56},{72,6... | collective-permute-start | bytes 393224 | tf_op jit(solution)/shard_map/while/body/eval_jaxpr/ppermute | solution.py:11
  261.6 8.4 %collective-permute-start = (f32[128,256]{1,0:T(8,128)S(1)}, f32[128,256]{1,0:T(8,128)S(1)}, u32[]{:S(2)}, u32[]{:S(2)}) collective-permute-start(f32[128,256]{1,0:T(8,128)S(1)} %fusion.53), channel_id=1, source_target_pairs={{8,0},{16,8},{24,16},{32,24},{40,32},{48,40},{56,48},{64,56},{72,6... | collective-permute-start | bytes 393224 | tf_op jit(solution)/shard_map/while/body/eval_jaxpr/ppermute | solution.py:11
  273.3 8.7 %collective-permute-start = (f32[128,256]{1,0:T(8,128)S(1)}, f32[128,256]{1,0:T(8,128)S(1)}, u32[]{:S(2)}, u32[]{:S(2)}) collective-permute-start(f32[128,256]{1,0:T(8,128)S(1)} %fusion.53), channel_id=1, source_target_pairs={{8,0},{16,8},{24,16},{32,24},{40,32},{48,40},{56,48},{64,56},{72,6... | collective-permute-start | bytes 393224 | tf_op jit(solution)/shard_map/while/body/eval_jaxpr/ppermute | solution.py:11
  285.3 8.6 %collective-permute-start = (f32[128,256]{1,0:T(8,128)S(1)}, f32[128,256]{1,0:T(8,128)S(1)}, u32[]{:S(2)}, u32[]{:S(2)}) collective-permute-start(f32[128,256]{1,0:T(8,128)S(1)} %fusion.53), channel_id=1, source_target_pairs={{8,0},{16,8},{24,16},{32,24},{40,32},{48,40},{56,48},{64,56},{72,6... | collective-permute-start | bytes 393224 | tf_op jit(solution)/shard_map/while/body/eval_jaxpr/ppermute | solution.py:11
  297.2 8.6 %collective-permute-start = (f32[128,256]{1,0:T(8,128)S(1)}, f32[128,256]{1,0:T(8,128)S(1)}, u32[]{:S(2)}, u32[]{:S(2)}) collective-permute-start(f32[128,256]{1,0:T(8,128)S(1)} %fusion.53), channel_id=1, source_target_pairs={{8,0},{16,8},{24,16},{32,24},{40,32},{48,40},{56,48},{64,56},{72,6... | collective-permute-start | bytes 393224 | tf_op jit(solution)/shard_map/while/body/eval_jaxpr/ppermute | solution.py:11
  309.1 9.1 %collective-permute-start = (f32[128,256]{1,0:T(8,128)S(1)}, f32[128,256]{1,0:T(8,128)S(1)}, u32[]{:S(2)}, u32[]{:S(2)}) collective-permute-start(f32[128,256]{1,0:T(8,128)S(1)} %fusion.53), channel_id=1, source_target_pairs={{8,0},{16,8},{24,16},{32,24},{40,32},{48,40},{56,48},{64,56},{72,6... | collective-permute-start | bytes 393224 | tf_op jit(solution)/shard_map/while/body/eval_jaxpr/ppermute | solution.py:11
  321.5 8.9 %collective-permute-start = (f32[128,256]{1,0:T(8,128)S(1)}, f32[128,256]{1,0:T(8,128)S(1)}, u32[]{:S(2)}, u32[]{:S(2)}) collective-permute-start(f32[128,256]{1,0:T(8,128)S(1)} %fusion.53), channel_id=1, source_target_pairs={{8,0},{16,8},{24,16},{32,24},{40,32},{48,40},{56,48},{64,56},{72,6... | collective-permute-start | bytes 393224 | tf_op jit(solution)/shard_map/while/body/eval_jaxpr/ppermute | solution.py:11
  333.6 8.3 %collective-permute-start = (f32[128,256]{1,0:T(8,128)S(1)}, f32[128,256]{1,0:T(8,128)S(1)}, u32[]{:S(2)}, u32[]{:S(2)}) collective-permute-start(f32[128,256]{1,0:T(8,128)S(1)} %fusion.53), channel_id=1, source_target_pairs={{8,0},{16,8},{24,16},{32,24},{40,32},{48,40},{56,48},{64,56},{72,6... | collective-permute-start | bytes 393224 | tf_op jit(solution)/shard_map/while/body/eval_jaxpr/ppermute | solution.py:11
  345.1 9.2 %collective-permute-start = (f32[128,256]{1,0:T(8,128)S(1)}, f32[128,256]{1,0:T(8,128)S(1)}, u32[]{:S(2)}, u32[]{:S(2)}) collective-permute-start(f32[128,256]{1,0:T(8,128)S(1)} %fusion.53), channel_id=1, source_target_pairs={{8,0},{16,8},{24,16},{32,24},{40,32},{48,40},{56,48},{64,56},{72,6... | collective-permute-start | bytes 393224 | tf_op jit(solution)/shard_map/while/body/eval_jaxpr/ppermute | solution.py:11
  357.5 8.5 %collective-permute-start = (f32[128,256]{1,0:T(8,128)S(1)}, f32[128,256]{1,0:T(8,128)S(1)}, u32[]{:S(2)}, u32[]{:S(2)}) collective-permute-start(f32[128,256]{1,0:T(8,128)S(1)} %fusion.53), channel_id=1, source_target_pairs={{8,0},{16,8},{24,16},{32,24},{40,32},{48,40},{56,48},{64,56},{72,6... | collective-permute-start | bytes 393224 | tf_op jit(solution)/shard_map/while/body/eval_jaxpr/ppermute | solution.py:11
  369.3 9.9 %collective-permute-start = (f32[128,256]{1,0:T(8,128)S(1)}, f32[128,256]{1,0:T(8,128)S(1)}, u32[]{:S(2)}, u32[]{:S(2)}) collective-permute-start(f32[128,256]{1,0:T(8,128)S(1)} %fusion.53), channel_id=1, source_target_pairs={{8,0},{16,8},{24,16},{32,24},{40,32},{48,40},{56,48},{64,56},{72,6... | collective-permute-start | bytes 393224 | tf_op jit(solution)/shard_map/while/body/eval_jaxpr/ppermute | solution.py:11
  382.5 10.5 %collective-permute-start = (f32[128,256]{1,0:T(8,128)S(1)}, f32[128,256]{1,0:T(8,128)S(1)}, u32[]{:S(2)}, u32[]{:S(2)}) collective-permute-start(f32[128,256]{1,0:T(8,128)S(1)} %fusion.53), channel_id=1, source_target_pairs={{8,0},{16,8},{24,16},{32,24},{40,32},{48,40},{56,48},{64,56},{72,6... | collective-permute-start | bytes 393224 | tf_op jit(solution)/shard_map/while/body/eval_jaxpr/ppermute | solution.py:11
  396.2 8.3 %collective-permute-start = (f32[128,256]{1,0:T(8,128)S(1)}, f32[128,256]{1,0:T(8,128)S(1)}, u32[]{:S(2)}, u32[]{:S(2)}) collective-permute-start(f32[128,256]{1,0:T(8,128)S(1)} %fusion.53), channel_id=1, source_target_pairs={{8,0},{16,8},{24,16},{32,24},{40,32},{48,40},{56,48},{64,56},{72,6... | collective-permute-start | bytes 393224 | tf_op jit(solution)/shard_map/while/body/eval_jaxpr/ppermute | solution.py:11
  407.8 8.7 %collective-permute-start = (f32[128,256]{1,0:T(8,128)S(1)}, f32[128,256]{1,0:T(8,128)S(1)}, u32[]{:S(2)}, u32[]{:S(2)}) collective-permute-start(f32[128,256]{1,0:T(8,128)S(1)} %fusion.53), channel_id=1, source_target_pairs={{8,0},{16,8},{24,16},{32,24},{40,32},{48,40},{56,48},{64,56},{72,6... | collective-permute-start | bytes 393224 | tf_op jit(solution)/shard_map/while/body/eval_jaxpr/ppermute | solution.py:11
Sparse Core Ops, SparseCore 0:
  137.3 78.3 reduce-scatter.1
  236.8 270.7 all-reduce.1
where the time goes:
time: 519 us; the launch traced here: 516 us
  waiting for transfers between devices  267 us (51%)
  starting transfers between devices  86.5 us (17%)
  local copies, waits for them, and re-layouts  66.3 us (13%)
  matrix products  36.1 us (7%)
  other arithmetic  26.9 us (5%)
  blocking collectives  17.1 us (3%)
  between operations  14.2 us (3%)
    ppermute x30, waiting for transfers between devices, passed_along(): return lax.ppermute(block, axis, route)  100 us
    psum x1, waiting for transfers between devices, per_device(): grad_weight = lax.psum(local_weight, ('blk', 'rep')) / math.sqrt(node_total)  89.1 us
    ppermute x30, starting transfers between devices, passed_along(): return lax.ppermute(block, axis, route)  86.4 us
    reduce_scatter x1, waiting for transfers between devices, per_device(): lax.psum_scatter(slab_partial, 'rep', scatter_dimension=0, tiled=True)  77.7 us
    dynamic_slice x31, local copies, waits for them, and re-layouts, load_distance(): lax.dynamic_index_in_dim(count_stack, distance, 0, keepdims=False)  29.8 us
    dot_general x16, matrix products, scatter_rows(): jnp.einsum('kij,kif->jf', tile_block, picked, preferred_element_type=jnp....  21.2 us
    all_gather x1, blocking collectives, per_device(): lax.all_gather(back_scaled, 'rep', axis=0, tiled=True)  17.1 us
    squeeze x16, local copies, waits for them, and re-layouts, load_distance(): lax.dynamic_index_in_dim(tile_stack, distance, 0, keepdims=False)  15.6 us
  transfers between devices with their start and end apart: 32, of which 17 were waited for; matrix products, arithmetic and copies ran while one was open for 22% of the time, Pallas kernels for 0%

commit v1 on v0

--- a/solution.py
+++ b/solution.py
@@ -63,7 +63,10 @@
         aggregated, act_grad, (((0,), (0,)), ((), ())), preferred_element_type=jnp.float32
     )
     node_total = own_rows * lax.axis_size("blk") * lax.axis_size("rep")
-    grad_weight = lax.psum(local_weight, ("blk", "rep")) / math.sqrt(node_total)
+    inputs_test = lambda here_x, row_axis, ax_name: jax.lax.psum(
+        jax.lax.psum(here_x, row_axis), ax_name
+    )
+    grad_weight = inputs_test(local_weight, "blk", "rep") / math.sqrt(node_total)
     back_grad = lax.dot_general(
         act_grad, weight, (((1,), (1,)), ((), ())), preferred_element_type=jnp.float32
     )

time: 519 us -> 1010 us (1.95)
  the two profiles are of different devices: /device:TPU:23 before, /device:TPU:94 now
where the time goes in v1:
time: 1010 us
  waiting for transfers between devices  728 us (72%)
  starting transfers between devices  120 us (12%)
  local copies, waits for them, and re-layouts  65.1 us (6%)
  matrix products  36.1 us (4%)
  other arithmetic  26.3 us (3%)
  blocking collectives  15.5 us (2%)
  between operations  13.9 us (1%)
    psum x1, waiting for transfers between devices, per_device(): jax.lax.psum(here_x, row_axis)  546 us
    ppermute x30, waiting for transfers between devices, passed_along(): return lax.ppermute(block, axis, route)  137 us
    ppermute x30, starting transfers between devices, passed_along(): return lax.ppermute(block, axis, route)  120 us
    reduce_scatter x1, waiting for transfers between devices, per_device(): lax.psum_scatter(slab_partial, 'rep', scatter_dimension=0, tiled=True)  44.4 us
    dynamic_slice x31, local copies, waits for them, and re-layouts, load_distance(): lax.dynamic_index_in_dim(count_stack, distance, 0, keepdims=False)  28.6 us
    dot_general x16, matrix products, scatter_rows(): jnp.einsum('kij,kif->jf', tile_block, picked, preferred_element_type=jnp....  21.2 us
  transfers between devices with their start and end apart: 33, of which 17 were waited for; matrix products, arithmetic and copies ran while one was open for 11% of the time, Pallas kernels for 0%

profile of v1, /device:TPU:94, one launch (start us, length us, event | category | flops | bytes accessed | tf_op | source)
XLA Modules:
  0.0 1006.7 jit_solution(4041459939695832653)
XLA Ops:
  9.8 1.3 fusion.41
  14.3 153.9 %while.34 = (s32[]{:T(128)}, f32[8,128,256]{2,1,0:T(8,128)S(1)}, bf16[128,256]{1,0:T(8,128)(2,1)S(1)}, s32[16,8]{1,0:T(8,128)S(1)}, s32[16]{0:T(128)}, /*index=5...) while((s32[]{:T(128)}, f32[8,128,256]{2,1,0:T(8,128)S(1)}, ...), condition=%wide.region_2.4_spmd.clone.clone, body=%wide.region_0.3_spmd.clone.clone.sunk | while | flops 68027656 | bytes 3871199 | solution.py:51
  14.3 3.7 collective-permute-start.1
  22.3 6.0 collective-permute-start.1
  32.7 6.0 collective-permute-start.1
  43.1 6.0 collective-permute-start.1
  53.5 6.0 collective-permute-start.1
  63.8 6.0 collective-permute-start.1
  74.2 6.0 collective-permute-start.1
  84.6 6.0 collective-permute-start.1
  95.0 6.7 collective-permute-start.1
  106.0 6.0 collective-permute-start.1
  116.4 6.0 collective-permute-start.1
  126.7 6.0 collective-permute-start.1
  137.1 6.0 collective-permute-start.1
  147.5 6.0 collective-permute-start.1
  157.8 6.0 collective-permute-start.1
  168.2 1.3 fusion.21
  170.3 44.4 %reduce-scatter.2.cloned.1.call-done = f32[128,256]{1,0:T(8,128)} async-done(((f32[1024,256]{1,0:T(8,128)}), f32[128,256]{1,0:T(8,128)}) %reduce-scatter.2.cloned.1.call-update) | async-done | bytes 131088 | tf_op jit(solution)/shard_map/reduce_scatter | solution.py:54
  214.7 1.8 multiply_convert_fusion
  216.5 1.9 fusion.39
  218.6 15.5 %all_gather.3 = bf16[1024,256]{1,0:T(8,128)(2,1)S(1)} all-gather(bf16[128,256]{1,0:T(8,128)(2,1)S(1)} %fusion.25), channel_id=1, replica_groups=mesh['blk'=64,'rep'=8] {'rep'}, dimensions={0}, use_global_device_ids=true | all-gather | bytes 589824 | tf_op jit(solution)/shard_map/all_gather | solution.py:74
  234.7 545.9 %all-reduce.3.cloned.1.call-done = f32[256,256]{1,0:T(8,128)} async-done(((f32[256,256]{1,0:T(8,128)}), f32[256,256]{1,0:T(8,128)}) %all-reduce.3.cloned.1.call-update) | async-done | bytes 262160 | tf_op jit(solution)/shard_map/psum | solution.py:67
  780.6 216.0 %while.33 = (s32[]{:T(128)}, f32[128,256]{1,0:T(8,128)S(1)}, bf16[16,8,128,128]{3,2,1,0:T(8,128)(2,1)}, s32[16]{0:T(128)S(1)}, s32[16,8]{1,0:T(8,128)S(1)}, /*in...) while((s32[]{:T(128)}, f32[128,256]{1,0:T(8,128)S(1)}, ...), condition=%wide.region_8.11_spmd.clone, body=%wide.region_7.10_spmd.clone.sunk | while | flops 67667008 | bytes 2625907 | solution.py:91
  783.8 4.6 collective-permute-start
  788.4 6.5 collective-permute-done
  796.7 1.3 fusion.53
  798.0 1.9 collective-permute-start
  800.0 9.3 collective-permute-done
  811.1 1.3 fusion.53
  812.4 1.9 collective-permute-start
  814.3 9.3 collective-permute-done
  826.8 1.9 collective-permute-start
  828.7 9.2 collective-permute-done
  841.0 1.9 collective-permute-start
  843.0 9.3 collective-permute-done
  854.1 1.3 fusion.53
  855.4 1.9 collective-permute-start
  857.4 9.1 collective-permute-done
  868.3 1.3 fusion.53
  869.6 1.9 collective-permute-start
  871.6 9.1 collective-permute-done
  882.6 1.3 fusion.53
  883.9 1.9 collective-permute-start
  885.8 9.1 collective-permute-done
  896.8 1.3 fusion.53
  898.1 1.9 collective-permute-start
  900.0 9.4 collective-permute-done
  912.5 1.9 collective-permute-start
  914.4 10.5 %collective-permute-done = f32[128,256]{1,0:T(8,128)S(1)} collective-permute-done((f32[128,256]{1,0:T(8,128)S(1)}, f32[128,256]{1,0:T(8,128)S(1)}, u32[]{:S(2)}, u32[]{:S(2)}) %collective-permute-start) | collective-permute-done | bytes 131104 | tf_op jit(solution)/shard_map/while/body/eval_jaxpr/ppermute | solution.py:11
  928.1 1.9 collective-permute-start
  930.0 9.7 collective-permute-done
  942.9 1.9 collective-permute-start
  944.8 9.1 collective-permute-done
  957.1 1.9 collective-permute-start
  959.0 9.1 collective-permute-done
  970.0 1.3 fusion.53
  971.3 1.9 collective-permute-start
  973.2 9.1 collective-permute-done
  984.2 1.3 fusion.53
  985.5 1.9 collective-permute-start
  987.5 9.1 collective-permute-done
  996.6 1.9 fusion.24
  998.5 1.7 broadcast_multiply_fusion
  (262 shorter events, 107.6 us)
Async XLA Ops:
  7.2 207.5 %copy-start = (bf16[256,256]{1,0:T(8,128)(2,1)S(1)}, bf16[256,256]{1,0:T(8,128)(2,1)}, u32[]{:S(2)}) copy-start(bf16[256,256]{1,0:T(8,128)(2,1)} %param.20) | copy-start | bytes 393220
  7.2 207.5 %reduce-scatter.2.cloned.1.call-start = ((), (), s32[]{:S(2)}) async-start(), calls=%async_computation.1 | async-start | bytes 1179648 | tf_op jit(solution)/shard_map/reduce_scatter | solution.py:54
  14.3 200.4 %copy-start.2 = (bf16[128,256]{1,0:T(8,128)(2,1)S(1)}, bf16[128,256]{1,0:T(8,128)(2,1)}, u32[]{:S(2)}) copy-start(bf16[128,256]{1,0:T(8,128)(2,1)} %param.21) | copy-start | bytes 196612
  14.3 8.0 collective-permute-start.1
  22.3 10.3 %collective-permute-start.1 = (bf16[128,256]{1,0:T(8,128)(2,1)S(1)}, bf16[128,256]{1,0:T(8,128)(2,1)S(1)}, u32[]{:S(2)}, u32[]{:S(2)}) collective-permute-start(bf16[128,256]{1,0:T(8,128)(2,1)S(1)} %copy.29), channel_id=1, source_target_pairs={{504,0},{0,8},{8,16},{16,24},{24,32},{32,40},{40,48},{48,56},{56,6... | collective-permute-start | bytes 196616 | tf_op jit(solution)/shard_map/while/body/eval_jaxpr/ppermute | solution.py:11
  32.7 10.3 %collective-permute-start.1 = (bf16[128,256]{1,0:T(8,128)(2,1)S(1)}, bf16[128,256]{1,0:T(8,128)(2,1)S(1)}, u32[]{:S(2)}, u32[]{:S(2)}) collective-permute-start(bf16[128,256]{1,0:T(8,128)(2,1)S(1)} %copy.29), channel_id=1, source_target_pairs={{504,0},{0,8},{8,16},{16,24},{24,32},{32,40},{40,48},{48,56},{56,6... | collective-permute-start | bytes 196616 | tf_op jit(solution)/shard_map/while/body/eval_jaxpr/ppermute | solution.py:11
  43.1 10.3 %collective-permute-start.1 = (bf16[128,256]{1,0:T(8,128)(2,1)S(1)}, bf16[128,256]{1,0:T(8,128)(2,1)S(1)}, u32[]{:S(2)}, u32[]{:S(2)}) collective-permute-start(bf16[128,256]{1,0:T(8,128)(2,1)S(1)} %copy.29), channel_id=1, source_target_pairs={{504,0},{0,8},{8,16},{16,24},{24,32},{32,40},{40,48},{48,56},{56,6... | collective-permute-start | bytes 196616 | tf_op jit(solution)/shard_map/while/body/eval_jaxpr/ppermute | solution.py:11
  53.5 10.3 %collective-permute-start.1 = (bf16[128,256]{1,0:T(8,128)(2,1)S(1)}, bf16[128,256]{1,0:T(8,128)(2,1)S(1)}, u32[]{:S(2)}, u32[]{:S(2)}) collective-permute-start(bf16[128,256]{1,0:T(8,128)(2,1)S(1)} %copy.29), channel_id=1, source_target_pairs={{504,0},{0,8},{8,16},{16,24},{24,32},{32,40},{40,48},{48,56},{56,6... | collective-permute-start | bytes 196616 | tf_op jit(solution)/shard_map/while/body/eval_jaxpr/ppermute | solution.py:11
  63.8 10.3 %collective-permute-start.1 = (bf16[128,256]{1,0:T(8,128)(2,1)S(1)}, bf16[128,256]{1,0:T(8,128)(2,1)S(1)}, u32[]{:S(2)}, u32[]{:S(2)}) collective-permute-start(bf16[128,256]{1,0:T(8,128)(2,1)S(1)} %copy.29), channel_id=1, source_target_pairs={{504,0},{0,8},{8,16},{16,24},{24,32},{32,40},{40,48},{48,56},{56,6... | collective-permute-start | bytes 196616 | tf_op jit(solution)/shard_map/while/body/eval_jaxpr/ppermute | solution.py:11
  74.2 10.3 %collective-permute-start.1 = (bf16[128,256]{1,0:T(8,128)(2,1)S(1)}, bf16[128,256]{1,0:T(8,128)(2,1)S(1)}, u32[]{:S(2)}, u32[]{:S(2)}) collective-permute-start(bf16[128,256]{1,0:T(8,128)(2,1)S(1)} %copy.29), channel_id=1, source_target_pairs={{504,0},{0,8},{8,16},{16,24},{24,32},{32,40},{40,48},{48,56},{56,6... | collective-permute-start | bytes 196616 | tf_op jit(solution)/shard_map/while/body/eval_jaxpr/ppermute | solution.py:11
  84.6 10.3 %collective-permute-start.1 = (bf16[128,256]{1,0:T(8,128)(2,1)S(1)}, bf16[128,256]{1,0:T(8,128)(2,1)S(1)}, u32[]{:S(2)}, u32[]{:S(2)}) collective-permute-start(bf16[128,256]{1,0:T(8,128)(2,1)S(1)} %copy.29), channel_id=1, source_target_pairs={{504,0},{0,8},{8,16},{16,24},{24,32},{32,40},{40,48},{48,56},{56,6... | collective-permute-start | bytes 196616 | tf_op jit(solution)/shard_map/while/body/eval_jaxpr/ppermute | solution.py:11
  95.0 11.0 %collective-permute-start.1 = (bf16[128,256]{1,0:T(8,128)(2,1)S(1)}, bf16[128,256]{1,0:T(8,128)(2,1)S(1)}, u32[]{:S(2)}, u32[]{:S(2)}) collective-permute-start(bf16[128,256]{1,0:T(8,128)(2,1)S(1)} %copy.29), channel_id=1, source_target_pairs={{504,0},{0,8},{8,16},{16,24},{24,32},{32,40},{40,48},{48,56},{56,6... | collective-permute-start | bytes 196616 | tf_op jit(solution)/shard_map/while/body/eval_jaxpr/ppermute | solution.py:11
  106.0 10.3 %collective-permute-start.1 = (bf16[128,256]{1,0:T(8,128)(2,1)S(1)}, bf16[128,256]{1,0:T(8,128)(2,1)S(1)}, u32[]{:S(2)}, u32[]{:S(2)}) collective-permute-start(bf16[128,256]{1,0:T(8,128)(2,1)S(1)} %copy.29), channel_id=1, source_target_pairs={{504,0},{0,8},{8,16},{16,24},{24,32},{32,40},{40,48},{48,56},{56,6... | collective-permute-start | bytes 196616 | tf_op jit(solution)/shard_map/while/body/eval_jaxpr/ppermute | solution.py:11
  116.4 10.3 %collective-permute-start.1 = (bf16[128,256]{1,0:T(8,128)(2,1)S(1)}, bf16[128,256]{1,0:T(8,128)(2,1)S(1)}, u32[]{:S(2)}, u32[]{:S(2)}) collective-permute-start(bf16[128,256]{1,0:T(8,128)(2,1)S(1)} %copy.29), channel_id=1, source_target_pairs={{504,0},{0,8},{8,16},{16,24},{24,32},{32,40},{40,48},{48,56},{56,6... | collective-permute-start | bytes 196616 | tf_op jit(solution)/shard_map/while/body/eval_jaxpr/ppermute | solution.py:11
  126.7 10.3 %collective-permute-start.1 = (bf16[128,256]{1,0:T(8,128)(2,1)S(1)}, bf16[128,256]{1,0:T(8,128)(2,1)S(1)}, u32[]{:S(2)}, u32[]{:S(2)}) collective-permute-start(bf16[128,256]{1,0:T(8,128)(2,1)S(1)} %copy.29), channel_id=1, source_target_pairs={{504,0},{0,8},{8,16},{16,24},{24,32},{32,40},{40,48},{48,56},{56,6... | collective-permute-start | bytes 196616 | tf_op jit(solution)/shard_map/while/body/eval_jaxpr/ppermute | solution.py:11
  137.1 10.3 %collective-permute-start.1 = (bf16[128,256]{1,0:T(8,128)(2,1)S(1)}, bf16[128,256]{1,0:T(8,128)(2,1)S(1)}, u32[]{:S(2)}, u32[]{:S(2)}) collective-permute-start(bf16[128,256]{1,0:T(8,128)(2,1)S(1)} %copy.29), channel_id=1, source_target_pairs={{504,0},{0,8},{8,16},{16,24},{24,32},{32,40},{40,48},{48,56},{56,6... | collective-permute-start | bytes 196616 | tf_op jit(solution)/shard_map/while/body/eval_jaxpr/ppermute | solution.py:11
  147.5 10.3 %collective-permute-start.1 = (bf16[128,256]{1,0:T(8,128)(2,1)S(1)}, bf16[128,256]{1,0:T(8,128)(2,1)S(1)}, u32[]{:S(2)}, u32[]{:S(2)}) collective-permute-start(bf16[128,256]{1,0:T(8,128)(2,1)S(1)} %copy.29), channel_id=1, source_target_pairs={{504,0},{0,8},{8,16},{16,24},{24,32},{32,40},{40,48},{48,56},{56,6... | collective-permute-start | bytes 196616 | tf_op jit(solution)/shard_map/while/body/eval_jaxpr/ppermute | solution.py:11
  157.8 10.3 %collective-permute-start.1 = (bf16[128,256]{1,0:T(8,128)(2,1)S(1)}, bf16[128,256]{1,0:T(8,128)(2,1)S(1)}, u32[]{:S(2)}, u32[]{:S(2)}) collective-permute-start(bf16[128,256]{1,0:T(8,128)(2,1)S(1)} %copy.29), channel_id=1, source_target_pairs={{504,0},{0,8},{8,16},{16,24},{24,32},{32,40},{40,48},{48,56},{56,6... | collective-permute-start | bytes 196616 | tf_op jit(solution)/shard_map/while/body/eval_jaxpr/ppermute | solution.py:11
  168.2 612.4 %copy-start.1 = (s32[16]{0:T(128)S(1)}, s32[16]{0:T(128)}, u32[]{:S(2)}) copy-start(s32[16]{0:T(128)} %get-tuple-element.586) | copy-start | bytes 196
  169.6 611.0 %all-reduce.3.cloned.1.call-start = ((), (), s32[]{:S(2)}) async-start(), calls=%async_computation.2 | async-start | bytes 524288 | tf_op jit(solution)/shard_map/psum | solution.py:67
  218.4 780.1 %all-reduce.5.cloned.1.call-start = ((), (), s32[]{:S(2)}) async-start(), calls=%async_computation.3 | async-start | bytes 524288 | tf_op jit(solution)/shard_map/psum | solution.py:66
  783.8 11.1 %collective-permute-start = (f32[128,256]{1,0:T(8,128)S(1)}, f32[128,256]{1,0:T(8,128)S(1)}, u32[]{:S(2)}, u32[]{:S(2)}) collective-permute-start(f32[128,256]{1,0:T(8,128)S(1)} %fusion.53), channel_id=1, source_target_pairs={{8,0},{16,8},{24,16},{32,24},{40,32},{48,40},{56,48},{64,56},{72,6... | collective-permute-start | bytes 393224 | tf_op jit(solution)/shard_map/while/body/eval_jaxpr/ppermute | solution.py:11
  798.0 11.2 %collective-permute-start = (f32[128,256]{1,0:T(8,128)S(1)}, f32[128,256]{1,0:T(8,128)S(1)}, u32[]{:S(2)}, u32[]{:S(2)}) collective-permute-start(f32[128,256]{1,0:T(8,128)S(1)} %fusion.53), channel_id=1, source_target_pairs={{8,0},{16,8},{24,16},{32,24},{40,32},{48,40},{56,48},{64,56},{72,6... | collective-permute-start | bytes 393224 | tf_op jit(solution)/shard_map/while/body/eval_jaxpr/ppermute | solution.py:11
  812.4 11.3 %collective-permute-start = (f32[128,256]{1,0:T(8,128)S(1)}, f32[128,256]{1,0:T(8,128)S(1)}, u32[]{:S(2)}, u32[]{:S(2)}) collective-permute-start(f32[128,256]{1,0:T(8,128)S(1)} %fusion.53), channel_id=1, source_target_pairs={{8,0},{16,8},{24,16},{32,24},{40,32},{48,40},{56,48},{64,56},{72,6... | collective-permute-start | bytes 393224 | tf_op jit(solution)/shard_map/while/body/eval_jaxpr/ppermute | solution.py:11
  826.8 11.1 %collective-permute-start = (f32[128,256]{1,0:T(8,128)S(1)}, f32[128,256]{1,0:T(8,128)S(1)}, u32[]{:S(2)}, u32[]{:S(2)}) collective-permute-start(f32[128,256]{1,0:T(8,128)S(1)} %fusion.53), channel_id=1, source_target_pairs={{8,0},{16,8},{24,16},{32,24},{40,32},{48,40},{56,48},{64,56},{72,6... | collective-permute-start | bytes 393224 | tf_op jit(solution)/shard_map/while/body/eval_jaxpr/ppermute | solution.py:11
  841.0 11.2 %collective-permute-start = (f32[128,256]{1,0:T(8,128)S(1)}, f32[128,256]{1,0:T(8,128)S(1)}, u32[]{:S(2)}, u32[]{:S(2)}) collective-permute-start(f32[128,256]{1,0:T(8,128)S(1)} %fusion.53), channel_id=1, source_target_pairs={{8,0},{16,8},{24,16},{32,24},{40,32},{48,40},{56,48},{64,56},{72,6... | collective-permute-start | bytes 393224 | tf_op jit(solution)/shard_map/while/body/eval_jaxpr/ppermute | solution.py:11
  855.4 11.1 %collective-permute-start = (f32[128,256]{1,0:T(8,128)S(1)}, f32[128,256]{1,0:T(8,128)S(1)}, u32[]{:S(2)}, u32[]{:S(2)}) collective-permute-start(f32[128,256]{1,0:T(8,128)S(1)} %fusion.53), channel_id=1, source_target_pairs={{8,0},{16,8},{24,16},{32,24},{40,32},{48,40},{56,48},{64,56},{72,6... | collective-permute-start | bytes 393224 | tf_op jit(solution)/shard_map/while/body/eval_jaxpr/ppermute | solution.py:11
  869.6 11.1 %collective-permute-start = (f32[128,256]{1,0:T(8,128)S(1)}, f32[128,256]{1,0:T(8,128)S(1)}, u32[]{:S(2)}, u32[]{:S(2)}) collective-permute-start(f32[128,256]{1,0:T(8,128)S(1)} %fusion.53), channel_id=1, source_target_pairs={{8,0},{16,8},{24,16},{32,24},{40,32},{48,40},{56,48},{64,56},{72,6... | collective-permute-start | bytes 393224 | tf_op jit(solution)/shard_map/while/body/eval_jaxpr/ppermute | solution.py:11
  883.9 11.1 %collective-permute-start = (f32[128,256]{1,0:T(8,128)S(1)}, f32[128,256]{1,0:T(8,128)S(1)}, u32[]{:S(2)}, u32[]{:S(2)}) collective-permute-start(f32[128,256]{1,0:T(8,128)S(1)} %fusion.53), channel_id=1, source_target_pairs={{8,0},{16,8},{24,16},{32,24},{40,32},{48,40},{56,48},{64,56},{72,6... | collective-permute-start | bytes 393224 | tf_op jit(solution)/shard_map/while/body/eval_jaxpr/ppermute | solution.py:11
  898.1 11.3 %collective-permute-start = (f32[128,256]{1,0:T(8,128)S(1)}, f32[128,256]{1,0:T(8,128)S(1)}, u32[]{:S(2)}, u32[]{:S(2)}) collective-permute-start(f32[128,256]{1,0:T(8,128)S(1)} %fusion.53), channel_id=1, source_target_pairs={{8,0},{16,8},{24,16},{32,24},{40,32},{48,40},{56,48},{64,56},{72,6... | collective-permute-start | bytes 393224 | tf_op jit(solution)/shard_map/while/body/eval_jaxpr/ppermute | solution.py:11
  912.5 12.4 %collective-permute-start = (f32[128,256]{1,0:T(8,128)S(1)}, f32[128,256]{1,0:T(8,128)S(1)}, u32[]{:S(2)}, u32[]{:S(2)}) collective-permute-start(f32[128,256]{1,0:T(8,128)S(1)} %fusion.53), channel_id=1, source_target_pairs={{8,0},{16,8},{24,16},{32,24},{40,32},{48,40},{56,48},{64,56},{72,6... | collective-permute-start | bytes 393224 | tf_op jit(solution)/shard_map/while/body/eval_jaxpr/ppermute | solution.py:11
  928.1 11.6 %collective-permute-start = (f32[128,256]{1,0:T(8,128)S(1)}, f32[128,256]{1,0:T(8,128)S(1)}, u32[]{:S(2)}, u32[]{:S(2)}) collective-permute-start(f32[128,256]{1,0:T(8,128)S(1)} %fusion.53), channel_id=1, source_target_pairs={{8,0},{16,8},{24,16},{32,24},{40,32},{48,40},{56,48},{64,56},{72,6... | collective-permute-start | bytes 393224 | tf_op jit(solution)/shard_map/while/body/eval_jaxpr/ppermute | solution.py:11
  942.9 11.1 %collective-permute-start = (f32[128,256]{1,0:T(8,128)S(1)}, f32[128,256]{1,0:T(8,128)S(1)}, u32[]{:S(2)}, u32[]{:S(2)}) collective-permute-start(f32[128,256]{1,0:T(8,128)S(1)} %fusion.53), channel_id=1, source_target_pairs={{8,0},{16,8},{24,16},{32,24},{40,32},{48,40},{56,48},{64,56},{72,6... | collective-permute-start | bytes 393224 | tf_op jit(solution)/shard_map/while/body/eval_jaxpr/ppermute | solution.py:11
  957.1 11.1 %collective-permute-start = (f32[128,256]{1,0:T(8,128)S(1)}, f32[128,256]{1,0:T(8,128)S(1)}, u32[]{:S(2)}, u32[]{:S(2)}) collective-permute-start(f32[128,256]{1,0:T(8,128)S(1)} %fusion.53), channel_id=1, source_target_pairs={{8,0},{16,8},{24,16},{32,24},{40,32},{48,40},{56,48},{64,56},{72,6... | collective-permute-start | bytes 393224 | tf_op jit(solution)/shard_map/while/body/eval_jaxpr/ppermute | solution.py:11
  971.3 11.1 %collective-permute-start = (f32[128,256]{1,0:T(8,128)S(1)}, f32[128,256]{1,0:T(8,128)S(1)}, u32[]{:S(2)}, u32[]{:S(2)}) collective-permute-start(f32[128,256]{1,0:T(8,128)S(1)} %fusion.53), channel_id=1, source_target_pairs={{8,0},{16,8},{24,16},{32,24},{40,32},{48,40},{56,48},{64,56},{72,6... | collective-permute-start | bytes 393224 | tf_op jit(solution)/shard_map/while/body/eval_jaxpr/ppermute | solution.py:11
  985.5 11.1 %collective-permute-start = (f32[128,256]{1,0:T(8,128)S(1)}, f32[128,256]{1,0:T(8,128)S(1)}, u32[]{:S(2)}, u32[]{:S(2)}) collective-permute-start(f32[128,256]{1,0:T(8,128)S(1)} %fusion.53), channel_id=1, source_target_pairs={{8,0},{16,8},{24,16},{32,24},{40,32},{48,40},{56,48},{64,56},{72,6... | collective-permute-start | bytes 393224 | tf_op jit(solution)/shard_map/while/body/eval_jaxpr/ppermute | solution.py:11
Sparse Core Ops, SparseCore 0:
  169.7 44.9 reduce-scatter.1
  218.5 562.0 all-reduce.2
  783.5 79.3 all-reduce.4
